TPU v7x, 128 devices: a whole 4x4x4 slice. The times are simulated.
128 devices in a mesh: slab: 32 (over y, z, core), col: 4 (over x).
Axes of the slice: x: 4, y: 4, z: 4, core: 2. Of those that a mesh axis runs over, the one named last changes fastest.
Arguments:
- input_map: float32 [64, 64, 192, 128], P('col', 'slab'), may hold values from -24 to 24
- output_map: float32 [64, 64, 192, 128], P('col', 'slab'), may hold values from -24 to 24
- region_ids: int32 [64, 192, 128], P('slab'), may hold values from 0 to 7
- region_cond: float32 [8], replicated, may hold values from 0.3 to 3
- shift_ids: int32 [2], replicated, may hold values from 0 to 7
Outputs:
- ctrl_factor: float32 [2, 64, 64, 192, 128], P(None, None, 'slab', 'col')
- obsv_factor: float32 [2, 64, 64, 192, 128], P(None, None, 'slab', 'col')
- cross_gram: float32 [128, 128], P('slab', 'col')
All inputs are finite; a program needn't handle non-finite values.
Results may differ from a plain program's by a relative error of at most 0.000098.
Values sent between devices are 32-bit elements; how exact they have to be, the bound alone decides.
A program may use at most 192 MiB of HBM per device.

v0:
```python
import math
import jax
import jax.numpy as jnp
from jax import lax
from jax.sharding import PartitionSpec as P

ADI = 2
STEPS = 3


def extended(block, sides, width):
    for axis, dim in sides:
        count = lax.axis_size(axis)
        forward = [(i, i + 1) for i in range(count - 1)]
        backward = [(target, source) for source, target in forward]
        low = lax.ppermute(
            lax.slice_in_dim(block, block.shape[dim] - width, None, axis=dim), axis, forward
        )
        high = lax.ppermute(lax.slice_in_dim(block, 0, width, axis=dim), axis, backward)
        block = jnp.concatenate([low, block, high], axis=dim)
    return block


def lookup(region_ids, region_cond):
    summed = jnp.zeros(region_ids.shape, jnp.float32)
    for region in range(region_cond.shape[0]):
        summed = summed + jnp.where(region_ids == region, region_cond[region], jnp.float32(0.0))
    return summed


def conduction(field_in, cond_ext):
    centre = field_in[:, 1:-1]
    cond_mid = cond_ext[1:-1]
    summed = 0.5 * (cond_mid + cond_ext[2:]) * (centre - field_in[:, 2:])
    summed = summed + 0.5 * (cond_mid + cond_ext[:-2]) * (centre - field_in[:, :-2])
    cond_y = jnp.pad(cond_mid, ((0, 0), (1, 1), (0, 0)))
    field_y = jnp.pad(centre, ((0, 0), (0, 0), (1, 1), (0, 0)))
    summed = summed + 0.5 * (cond_mid + cond_y[:, 2:]) * (centre - field_y[:, :, 2:])
    summed = summed + 0.5 * (cond_mid + cond_y[:, :-2]) * (centre - field_y[:, :, :-2])
    cond_z = jnp.pad(cond_mid, ((0, 0), (0, 0), (1, 1)))
    field_z = jnp.pad(centre, ((0, 0), (0, 0), (0, 0), (1, 1)))
    summed = summed + 0.5 * (cond_mid + cond_z[:, :, 2:]) * (centre - field_z[:, :, :, 2:])
    summed = summed + 0.5 * (cond_mid + cond_z[:, :, :-2]) * (centre - field_z[:, :, :, :-2])
    return summed


def bounds(shift_val, cond_max):
    high_eig = shift_val + 12.0 * cond_max
    mid_eig = 0.5 * (high_eig + shift_val)
    half_span = 0.5 * (high_eig - shift_val)
    return (mid_eig, half_span, mid_eig / half_span)


def solve_slabs(right_side, shift_val, cond_max, cond_ext):
    mid_eig, half_span, ratio_eig = bounds(shift_val, cond_max)
    rho_now = 1.0 / ratio_eig
    solution = jnp.zeros_like(right_side)
    residual = right_side
    direction = right_side / mid_eig
    for sweep_idx in range(STEPS - 1):
        solution = solution + direction
        padded = extended(direction, (("slab", 1),), 1)
        applied = conduction(padded, cond_ext) + shift_val * direction
        residual = residual - applied
        rho_next = 1.0 / (2.0 * ratio_eig - rho_now)
        direction = rho_next * rho_now * direction + 2.0 * rho_next / half_span * residual
        rho_now = rho_next
    return solution + direction


def run_segments(stacked, shifts, solver):
    factors = []
    current = stacked
    for segment_idx in range(ADI):
        shift_val = shifts[segment_idx]
        if segment_idx == 0:
            current = solver(stacked, shift_val)
        else:
            current = current - (shifts[segment_idx - 1] + shift_val) * solver(current, shift_val)
        factors.append(jnp.sqrt(2.0 * shift_val) * current)
    return jnp.stack(factors)


def body(input_map, output_map, region_ids, region_cond, shift_ids):
    col_local = input_map.shape[0]
    local_x = input_map.shape[1]
    cond_cells = lookup(region_ids, region_cond)
    cond_max = jnp.max(region_cond)
    shifts = 0.25 * jnp.exp2(shift_ids.astype(jnp.float32))
    total_x = local_x * lax.axis_size("slab")
    stacked = jnp.concatenate([input_map, output_map], 0)
    cond_ext = extended(cond_cells, (("slab", 0),), 1)
    factor_stack = run_segments(
        stacked, shifts, lambda rhs, shift_val: solve_slabs(rhs, shift_val, cond_max, cond_ext)
    )
    ctrl_local = factor_stack[:, :col_local]
    obsv_local = factor_stack[:, col_local:]
    ctrl_cols, obsv_cols = (
        lax.all_to_all(ctrl_local, "col", split_axis=3, concat_axis=1, tiled=True),
        lax.all_to_all(obsv_local, "col", split_axis=3, concat_axis=1, tiled=True),
    )
    row_count = ctrl_cols.shape[0] * ctrl_cols.shape[1]
    ctrl_flat = ctrl_cols.reshape(row_count, -1)
    obsv_flat = obsv_cols.reshape(row_count, -1)
    partial_value = lax.dot_general(
        ctrl_flat,
        obsv_flat,
        (((1,), (1,)), ((), ())),
        precision=lax.Precision.HIGHEST,
        preferred_element_type=jnp.float32,
    )
    cells_total = total_x * region_ids.shape[1] * region_ids.shape[2]
    norm_scale = 1.0 / math.sqrt(cells_total)
    whole_sum = lax.psum(partial_value, ("slab", "col"))
    tile_rows = row_count // lax.axis_size("slab")
    tile_cols = row_count // lax.axis_size("col")
    own_tile = lax.dynamic_slice(
        whole_sum,
        (lax.axis_index("slab") * tile_rows, lax.axis_index("col") * tile_cols),
        (tile_rows, tile_cols),
    )
    return (ctrl_cols, obsv_cols, own_tile * norm_scale)


def solution(mesh):
    placed = (
        P("col", "slab", None, None),
        P("col", "slab", None, None),
        P("slab", None, None),
        P(),
        P(),
    )
    return jax.shard_map(
        body,
        mesh=mesh,
        in_specs=placed,
        out_specs=(
            P(None, None, "slab", "col", None),
            P(None, None, "slab", "col", None),
            P("slab", "col"),
        ),
        check_vma=False,
    )
```

profile of v0, /device:TPU:1, one launch (start us, length us, event | category | flops | bytes accessed | tf_op | source)
XLA Modules:
  0.0 643.6 jit_solution(5252572299411760887)
XLA Ops:
  8.6 1.3 reduce_max.9
  11.8 3.9 constant_dynamic-update-slice_fusion.1
  15.7 1.9 constant_dynamic-update-slice_fusion
  17.6 3.2 broadcast_divide_fusion.1
  20.9 3.3 fusion.105
  24.2 1.3 copy-done.1
  25.4 3.3 collective-permute-start.1
  28.8 3.5 collective-permute-start.3
  33.0 5.2 select_add_fusion
  38.2 2.5 collective-permute-start
  40.7 3.1 collective-permute-start.2
  44.6 22.0 %collective-permute-done = f32[1,192,128]{2,1,0:T(8,128)S(1)} collective-permute-done((f32[1,192,128]{2,1,0:T(8,128)S(1)}, f32[1,192,128]{2,1,0:T(8,128)S(1)}, u32[]{:S(2)}, u32[]{:S(2)}) %collective-permute-start) | collective-permute-done | bytes 98336 | tf_op jit(solution)/shard_map/ppermute | solution.py:19
  66.6 1.2 collective-permute-done.2
  68.0 23.3 %multiply_add_fusion.1 = (f32[32,2,192,128]{3,2,1,0:T(8,128)S(1)}, f32[32,2,192,128]{3,2,1,0:T(8,128)}) fusion(f32[32,2,192,128]{3,2,1,0:T(8,128)} %copy-done.1, f32[]{:T(128)S(6)} %div.53, f32[]{:T(128)S(6)} %mul.354, f32[32,2,192,128]{3,2,1,0:T(8,128)} %constant_dynamic-update-slice_fusion, f32[]{:T(128)} %bitcast, ...), kind=kLoop, calls=%fused_computation.116 | loop fusion | flops 39321600 | bytes 32636940 | tf_op jit(solution)/shard_map/add | solution.py:66
  91.3 3.2 fusion.104
  94.6 1.4 copy-done.3
  95.9 1.9 collective-permute-start.4
  97.8 4.4 collective-permute-start.5
  103.6 32.0 %collective-permute-done.4 = f32[32,1,192,128]{3,2,1,0:T(8,128)} collective-permute-done((f32[32,1,192,128]{3,2,1,0:T(8,128)}, f32[32,1,192,128]{3,2,1,0:T(8,128)}, u32[]{:S(2)}, u32[]{:S(2)}) %collective-permute-start.4) | collective-permute-done | bytes 3145760 | tf_op jit(solution)/shard_map/ppermute | solution.py:19
  135.5 1.2 collective-permute-done.5
  136.7 26.0 %broadcast_divide_fusion = (f32[32,2,192,128]{3,2,1,0:T(8,128)S(1)}, f32[32,2,192,128]{3,2,1,0:T(8,128)}) fusion(f32[]{:T(128)S(6)} %mul.397, f32[32,2,192,128]{3,2,1,0:T(8,128)} %get-tuple-element.8, f32[32,2,192,128]{3,2,1,0:T(8,128)} %copy-done.3, f32[]{:T(128)} %bitcast, f32[2,192,128]{2,1,0:T(8,128)S(1)} %get-tuple-element.29, ...), kind=kLoop, calls=%fused_computation.117 | loop fusion | flops 45613056 | bytes 38928404 | tf_op jit(solution)/shard_map/div | solution.py:59
  162.7 3.8 fusion.103
  166.5 0.8 copy-done.2
  167.3 1.9 collective-permute-start.6
  169.2 4.4 collective-permute-start.7
  175.1 31.8 %collective-permute-done.6 = f32[32,1,192,128]{3,2,1,0:T(8,128)} collective-permute-done((f32[32,1,192,128]{3,2,1,0:T(8,128)}, f32[32,1,192,128]{3,2,1,0:T(8,128)}, u32[]{:S(2)}, u32[]{:S(2)}) %collective-permute-start.6) | collective-permute-done | bytes 3145760 | tf_op jit(solution)/shard_map/ppermute | solution.py:19
  207.0 1.2 collective-permute-done.7
  208.1 26.6 %multiply_add_fusion = (f32[32,2,192,128]{3,2,1,0:T(8,128)S(1)}, f32[32,2,192,128]{3,2,1,0:T(8,128)}, f32[1,32,2,192,128]{4,3,2,1,0:T(8,128)}) fusion(f32[]{:T(128)S(6)} %div.61, f32[]{:T(128)S(6)} %mul.400, f32[32,2,192,128]{3,2,1,0:T(8,128)} %get-tuple-element.6, f32[]{:T(128)S(6)} %mul.397, f32[32,2,192,128]{3,2,1,0:T(8,128)} %copy-done.2, f32[]{:T(128)} %bitcast.10, ...), kind=kLoop, calls=%fused_computation.114 | loop fusion | flops 42467328 | bytes 38928404 | tf_op jit(solution)/shard_map/add | solution.py:66
  234.7 3.8 fusion.102
  239.3 1.9 collective-permute-start.8
  241.2 4.6 collective-permute-start.9
  247.8 31.1 %collective-permute-done.8 = f32[32,1,192,128]{3,2,1,0:T(8,128)} collective-permute-done((f32[32,1,192,128]{3,2,1,0:T(8,128)}, f32[32,1,192,128]{3,2,1,0:T(8,128)}, u32[]{:S(2)}, u32[]{:S(2)}) %collective-permute-start.8) | collective-permute-done | bytes 3145760 | tf_op jit(solution)/shard_map/ppermute | solution.py:19
  278.9 1.2 collective-permute-done.9
  280.1 27.0 %fusion.47 = f32[1,32,2,192,128]{4,3,2,1,0:T(8,128)S(1)} fusion(f32[32,2,192,128]{3,2,1,0:T(8,128)} %get-tuple-element.6, f32[32,2,192,128]{3,2,1,0:T(8,128)} %get-tuple-element.4, f32[32,2,192,128]{3,2,1,0:T(8,128)} %copy-done, f32[32,1,192,128]{3,2,1,0:T(8,128)} %collective-permute-done.9, f32[32,1,192,128]{3,2,1,0:T(8,128)} %collective-permute-done.8, ...), kind=kLoop, calls=%fused_computation.65 | loop fusion | flops 48758784 | bytes 32636952 | tf_op jit(solution)/shard_map/stack | solution.py:81
  307.2 3.1 pad_maximum_fusion
  310.3 7.6 %copy.32 = f32[2,16,2,192,128]{4,2,1,0,3:T(2,128)} copy(f32[2,16,2,192,128]{4,3,2,1,0:T(8,128)S(1)} %get-tuple-element.10) | data formatting | bytes 12582912 | tf_op jit(solution)/shard_map/slice | solution.py:96
  317.9 5.3 all-to-all-start
  323.1 10.2 %copy.34 = f32[2,16,2,192,128]{4,2,1,0,3:T(2,128)} copy(f32[2,16,2,192,128]{4,3,2,1,0:T(8,128)} %get-tuple-element.9) | data formatting | bytes 12582912 | tf_op jit(solution)/shard_map/slice | solution.py:97
  333.4 51.1 %all-to-all-done = f32[2,16,2,192,128]{4,2,1,0,3:T(2,128)} async-done(((f32[2,16,2,192,128]{4,2,1,0,3:T(2,128)}), f32[2,16,2,192,128]{4,2,1,0,3:T(2,128)}, u32[]{:S(2)}, u32[]{:S(2)}) %all-to-all-start) | async-done | bytes 6291488 | tf_op jit(solution)/shard_map/all_to_all | solution.py:99
  384.5 5.2 all-to-all-start.1
  390.0 9.0 %copy.41 = f32[2,16,2,4,48,128]{5,4,2,1,3,0:T(8,128)} copy(f32[2,16,2,4,48,128]{5,2,1,0,4,3:T(2,128)} %bitcast.12) | data formatting | bytes 12582912 | tf_op jit(solution)/shard_map/all_to_all | solution.py:99
  399.0 7.5 %reshape.20 = f32[128,12288]{1,0:T(8,128)} reshape(f32[2,4,16,2,48,128]{5,4,3,2,1,0:T(8,128)} %bitcast.32) | data formatting | bytes 12582912 | tf_op jit(solution)/shard_map/reshape | solution.py:103
  406.5 25.3 %all-to-all-done.1 = f32[2,16,2,192,128]{4,2,1,0,3:T(2,128)} async-done(((f32[2,16,2,192,128]{4,2,1,0,3:T(2,128)}), f32[2,16,2,192,128]{4,2,1,0,3:T(2,128)}, u32[]{:S(2)}, u32[]{:S(2)}) %all-to-all-start.1) | async-done | bytes 6291488 | tf_op jit(solution)/shard_map/all_to_all | solution.py:100
  431.7 9.0 %copy.40 = f32[2,16,2,4,48,128]{5,4,2,1,3,0:T(8,128)} copy(f32[2,16,2,4,48,128]{5,2,1,0,4,3:T(2,128)} %bitcast.15) | data formatting | bytes 12582912 | tf_op jit(solution)/shard_map/all_to_all | solution.py:100
  440.8 7.4 %reshape.21 = f32[128,12288]{1,0:T(8,128)} reshape(f32[2,4,16,2,48,128]{5,4,3,2,1,0:T(8,128)} %bitcast.34) | data formatting | bytes 12582912 | tf_op jit(solution)/shard_map/reshape | solution.py:104
  448.2 8.8 %fusion.109 = f32[128,128]{1,0:T(8,128)} fusion(f32[128,12288]{1,0:T(8,128)} %reshape.20, f32[128,12288]{1,0:T(8,128)} %reshape.21), kind=kOutput, calls=%fused_computation.151 | convolution fusion | flops 2415919104 | bytes 12648448 | tf_op jit(solution)/shard_map/dot_general | solution.py:105
  457.1 178.4 %all-reduce.12.cloned.1.call-done = f32[128,128]{1,0:T(8,128)} async-done(((f32[128,128]{1,0:T(8,128)}), f32[128,128]{1,0:T(8,128)}) %all-reduce.12.cloned.1.call-update) | async-done | bytes 65552 | tf_op jit(solution)/shard_map/psum | solution.py:114
  635.4 1.3 dynamic-slice_multiply_fusion
  (22 shorter events, 3.4 us)
Async XLA Ops:
  7.2 8.6 %copy-start.5 = (f32[16,2,192,128]{3,2,1,0:T(8,128)S(1)}, f32[16,2,192,128]{3,2,1,0:T(8,128)}, u32[]{:S(2)}) copy-start(f32[16,2,192,128]{3,2,1,0:T(8,128)} %param.6) | copy-start | bytes 9437188
  20.9 4.6 copy-start.1
  20.9 11.4 %copy-start.7 = (f32[8]{0:T(128)S(1)}, f32[8]{0:T(128)}, u32[]{:S(2)}) copy-start(f32[8]{0:T(128)} %param.8) | copy-start | bytes 100
  20.9 12.1 %copy-start.6 = (s32[2,192,128]{2,1,0:T(8,128)S(1)}, s32[2,192,128]{2,1,0:T(8,128)}, u32[]{:S(2)}) copy-start(s32[2,192,128]{2,1,0:T(8,128)} %param.7) | copy-start | bytes 589828
  25.4 42.5 %collective-permute-start.1 = (f32[32,1,192,128]{3,2,1,0:T(8,128)}, f32[32,1,192,128]{3,2,1,0:T(8,128)}, u32[]{:S(2)}, u32[]{:S(2)}) collective-permute-start(f32[32,1,192,128]{3,2,1,0:T(8,128)} %get-tuple-element.22), channel_id=1, source_target_pairs={{4,0},{8,4},{12,8},{16,12},{20,16},{24,20},{28,24},{32,28},{36,32}... | collective-permute-start | bytes 9437192 | tf_op jit(solution)/shard_map/ppermute | solution.py:19
  28.8 39.2 %collective-permute-start.3 = (f32[32,1,192,128]{3,2,1,0:T(8,128)}, f32[32,1,192,128]{3,2,1,0:T(8,128)}, u32[]{:S(2)}, u32[]{:S(2)}) collective-permute-start(f32[32,1,192,128]{3,2,1,0:T(8,128)} %get-tuple-element.23), channel_id=1, source_target_pairs={{0,4},{4,8},{8,12},{12,16},{16,20},{20,24},{24,28},{28,32},{32,36}... | collective-permute-start | bytes 9437192 | tf_op jit(solution)/shard_map/ppermute | solution.py:16
  38.2 28.4 %collective-permute-start = (f32[1,192,128]{2,1,0:T(8,128)S(1)}, f32[1,192,128]{2,1,0:T(8,128)S(1)}, u32[]{:S(2)}, u32[]{:S(2)}) collective-permute-start(f32[1,192,128]{2,1,0:T(8,128)S(1)} %get-tuple-element.30), channel_id=1, source_target_pairs={{4,0},{8,4},{12,8},{16,12},{20,16},{24,20},{28,24},{32,28},{36,32}... | collective-permute-start | bytes 294920 | tf_op jit(solution)/shard_map/ppermute | solution.py:19
  40.7 27.1 %collective-permute-start.2 = (f32[1,192,128]{2,1,0:T(8,128)S(1)}, f32[1,192,128]{2,1,0:T(8,128)S(1)}, u32[]{:S(2)}, u32[]{:S(2)}) collective-permute-start(f32[1,192,128]{2,1,0:T(8,128)S(1)} %get-tuple-element.31), channel_id=1, source_target_pairs={{0,4},{4,8},{8,12},{12,16},{16,20},{20,24},{24,28},{28,32},{32,36}... | collective-permute-start | bytes 294920 | tf_op jit(solution)/shard_map/ppermute | solution.py:16
  91.3 4.6 copy-start.3
  95.9 39.6 %collective-permute-start.4 = (f32[32,1,192,128]{3,2,1,0:T(8,128)}, f32[32,1,192,128]{3,2,1,0:T(8,128)}, u32[]{:S(2)}, u32[]{:S(2)}) collective-permute-start(f32[32,1,192,128]{3,2,1,0:T(8,128)} %get-tuple-element.20), channel_id=1, source_target_pairs={{4,0},{8,4},{12,8},{16,12},{20,16},{24,20},{28,24},{32,28},{36,32}... | collective-permute-start | bytes 9437192 | tf_op jit(solution)/shard_map/ppermute | solution.py:19
  97.8 38.9 %collective-permute-start.5 = (f32[32,1,192,128]{3,2,1,0:T(8,128)}, f32[32,1,192,128]{3,2,1,0:T(8,128)}, u32[]{:S(2)}, u32[]{:S(2)}) collective-permute-start(f32[32,1,192,128]{3,2,1,0:T(8,128)} %get-tuple-element.21), channel_id=1, source_target_pairs={{0,4},{4,8},{8,12},{12,16},{16,20},{20,24},{24,28},{28,32},{32,36}... | collective-permute-start | bytes 9437192 | tf_op jit(solution)/shard_map/ppermute | solution.py:16
  162.7 4.6 copy-start.2
  167.3 39.6 %collective-permute-start.6 = (f32[32,1,192,128]{3,2,1,0:T(8,128)}, f32[32,1,192,128]{3,2,1,0:T(8,128)}, u32[]{:S(2)}, u32[]{:S(2)}) collective-permute-start(f32[32,1,192,128]{3,2,1,0:T(8,128)} %get-tuple-element.18), channel_id=1, source_target_pairs={{4,0},{8,4},{12,8},{16,12},{20,16},{24,20},{28,24},{32,28},{36,32}... | collective-permute-start | bytes 9437192 | tf_op jit(solution)/shard_map/ppermute | solution.py:19
  169.2 38.9 %collective-permute-start.7 = (f32[32,1,192,128]{3,2,1,0:T(8,128)}, f32[32,1,192,128]{3,2,1,0:T(8,128)}, u32[]{:S(2)}, u32[]{:S(2)}) collective-permute-start(f32[32,1,192,128]{3,2,1,0:T(8,128)} %get-tuple-element.19), channel_id=1, source_target_pairs={{0,4},{4,8},{8,12},{12,16},{16,20},{20,24},{24,28},{28,32},{32,36}... | collective-permute-start | bytes 9437192 | tf_op jit(solution)/shard_map/ppermute | solution.py:16
  234.7 4.6 copy-start
  239.3 39.6 %collective-permute-start.8 = (f32[32,1,192,128]{3,2,1,0:T(8,128)}, f32[32,1,192,128]{3,2,1,0:T(8,128)}, u32[]{:S(2)}, u32[]{:S(2)}) collective-permute-start(f32[32,1,192,128]{3,2,1,0:T(8,128)} %get-tuple-element.15), channel_id=1, source_target_pairs={{4,0},{8,4},{12,8},{16,12},{20,16},{24,20},{28,24},{32,28},{36,32}... | collective-permute-start | bytes 9437192 | tf_op jit(solution)/shard_map/ppermute | solution.py:19
  241.2 38.9 %collective-permute-start.9 = (f32[32,1,192,128]{3,2,1,0:T(8,128)}, f32[32,1,192,128]{3,2,1,0:T(8,128)}, u32[]{:S(2)}, u32[]{:S(2)}) collective-permute-start(f32[32,1,192,128]{3,2,1,0:T(8,128)} %get-tuple-element.16), channel_id=1, source_target_pairs={{0,4},{4,8},{8,12},{12,16},{16,20},{20,24},{24,28},{28,32},{32,36}... | collective-permute-start | bytes 9437192 | tf_op jit(solution)/shard_map/ppermute | solution.py:16
  280.1 27.0 %copy-start.4 = (f32[1,32,2,192,128]{4,3,2,1,0:T(8,128)S(1)}, f32[1,32,2,192,128]{4,3,2,1,0:T(8,128)}, u32[]{:S(2)}) copy-start(f32[1,32,2,192,128]{4,3,2,1,0:T(8,128)} %get-tuple-element.17) | copy-start | bytes 18874372
  317.9 66.6 %all-to-all-start = ((f32[2,16,2,192,128]{4,2,1,0,3:T(2,128)}), f32[2,16,2,192,128]{4,2,1,0,3:T(2,128)}, u32[]{:S(2)}, u32[]{:S(2)}) async-start(f32[2,16,2,192,128]{4,2,1,0,3:T(2,128)} %copy.32), calls=%async_computation | async-start | bytes 12582912 | tf_op jit(solution)/shard_map/all_to_all | solution.py:99
  384.5 47.3 %all-to-all-start.1 = ((f32[2,16,2,192,128]{4,2,1,0,3:T(2,128)}), f32[2,16,2,192,128]{4,2,1,0,3:T(2,128)}, u32[]{:S(2)}, u32[]{:S(2)}) async-start(f32[2,16,2,192,128]{4,2,1,0,3:T(2,128)} %copy.34), calls=%async_computation.1 | async-start | bytes 12582912 | tf_op jit(solution)/shard_map/all_to_all | solution.py:100
  389.7 245.7 %all-reduce.12.cloned.1.call-start = ((), (), s32[]{:S(2)}) async-start(), calls=%async_computation.2 | async-start | bytes 131072 | tf_op jit(solution)/shard_map/psum | solution.py:114
Sparse Core Ops, SparseCore 0:
  457.2 178.1 all-reduce.11
where the time goes:
time: 645 us; the launch traced here: 644 us
  waiting for transfers between devices  376 us (58%)
  other arithmetic  118 us (18%)
  local copies, waits for them, and re-layouts  76.2 us (12%)
  starting transfers between devices  42.3 us (7%)
  between operations  21.9 us (3%)
  matrix products  8.8 us (1%)
    psum x1, waiting for transfers between devices, body(): whole_sum = lax.psum(partial_value, ('slab', 'col'))  178 us
    ppermute x5, waiting for transfers between devices, extended(): lax.ppermute(lax.slice_in_dim(block, 0, width, axis=dim), axis, backward)  117 us
    all_to_all x1, waiting for transfers between devices, body(): lax.all_to_all(ctrl_local, 'col', split_axis=3, concat_axis=1, tiled=True)  51.1 us
    add x2, other arithmetic, solve_slabs(): rho_next * rho_now * direction + 2.0 * rho_next / half_span * residual  49.9 us
    another operation x2, other arithmetic, run_segments(): return jnp.stack(factors)  30.2 us
    div x2, other arithmetic, solve_slabs(): direction = right_side / mid_eig  29.2 us
    all_to_all x1, waiting for transfers between devices, body(): lax.all_to_all(obsv_local, 'col', split_axis=3, concat_axis=1, tiled=True)  25.3 us
    ppermute x5, starting transfers between devices, extended(): lax.ppermute(lax.slice_in_dim(block, block.shape[dim] - width, None, axis...  19.9 us
  transfers between devices with their start and end apart: 13, of which 11 were waited for; matrix products, arithmetic and copies ran while one was open for 5% of the time, Pallas kernels for 0%

commit v1 on v0

--- a/solution.py
+++ b/solution.py
@@ -111,7 +111,7 @@
     )
     cells_total = total_x * region_ids.shape[1] * region_ids.shape[2]
     norm_scale = 1.0 / math.sqrt(cells_total)
-    whole_sum = lax.psum(partial_value, ("slab", "col"))
+    whole_sum = jnp.sum(lax.all_gather(partial_value, axis_name=("slab", "col")), axis=0)
     tile_rows = row_count // lax.axis_size("slab")
     tile_cols = row_count // lax.axis_size("col")
     own_tile = lax.dynamic_slice(

time: 645 us -> 581 us (0.901)
  waiting for transfers between devices: 376 us -> 309 us
    psum x1 -> x0, waiting for transfers between devices: 178 us -> none  [body(): whole_sum = lax.psum(partial_value, ('slab', 'col'))]
    all_gather x0 -> x1, waiting for transfers between devices: none -> 111 us  [body(): lax.all_gather(partial_value, axis_name=('slab', 'col'))]
  transfers between devices with their start and end apart: 13 -> 13, of which waited for: 11 -> 11; matrix products, arithmetic and copies ran while one was open for 5% -> 6% of each run, Pallas kernels for 0% -> 0%
where the time goes in v1:
time: 581 us; the launch traced here: 579 us
  waiting for transfers between devices  309 us (53%)
  other arithmetic  121 us (21%)
  local copies, waits for them, and re-layouts  76.2 us (13%)
  starting transfers between devices  42.3 us (7%)
  between operations  21.9 us (4%)
  matrix products  8.8 us (2%)
    ppermute x5, waiting for transfers between devices, extended(): lax.ppermute(lax.slice_in_dim(block, 0, width, axis=dim), axis, backward)  117 us
    all_gather x1, waiting for transfers between devices, body(): lax.all_gather(partial_value, axis_name=('slab', 'col'))  111 us
    all_to_all x1, waiting for transfers between devices, body(): lax.all_to_all(ctrl_local, 'col', split_axis=3, concat_axis=1, tiled=True)  51.1 us
    add x2, other arithmetic, solve_slabs(): rho_next * rho_now * direction + 2.0 * rho_next / half_span * residual  49.9 us
    another operation x2, other arithmetic, run_segments(): return jnp.stack(factors)  30.2 us
    div x2, other arithmetic, solve_slabs(): direction = right_side / mid_eig  29.2 us
    all_to_all x1, waiting for transfers between devices, body(): lax.all_to_all(obsv_local, 'col', split_axis=3, concat_axis=1, tiled=True)  25.3 us
    ppermute x5, starting transfers between devices, extended(): lax.ppermute(lax.slice_in_dim(block, block.shape[dim] - width, None, axis...  19.9 us
  transfers between devices with their start and end apart: 13, of which 11 were waited for; matrix products, arithmetic and copies ran while one was open for 6% of the time, Pallas kernels for 0%

profile of v1, /device:TPU:1, one launch (start us, length us, event | category | flops | bytes accessed | tf_op | source)
XLA Modules:
  0.0 579.4 jit_solution(7154702397312808790)
XLA Ops:
  8.6 1.3 reduce_max.9
  11.8 3.9 constant_dynamic-update-slice_fusion.1
  15.7 1.9 constant_dynamic-update-slice_fusion
  17.6 3.2 broadcast_divide_fusion.1
  20.9 3.3 fusion.105
  24.2 1.3 copy-done.1
  25.4 3.3 collective-permute-start.1
  28.8 3.5 collective-permute-start.3
  33.0 5.2 select_add_fusion
  38.2 2.5 collective-permute-start
  40.7 3.1 collective-permute-start.2
  44.6 22.0 %collective-permute-done = f32[1,192,128]{2,1,0:T(8,128)S(1)} collective-permute-done((f32[1,192,128]{2,1,0:T(8,128)S(1)}, f32[1,192,128]{2,1,0:T(8,128)S(1)}, u32[]{:S(2)}, u32[]{:S(2)}) %collective-permute-start) | collective-permute-done | bytes 98336 | tf_op jit(solution)/shard_map/ppermute | solution.py:19
  66.6 1.2 collective-permute-done.2
  68.0 23.3 %multiply_add_fusion.1 = (f32[32,2,192,128]{3,2,1,0:T(8,128)S(1)}, f32[32,2,192,128]{3,2,1,0:T(8,128)}) fusion(f32[32,2,192,128]{3,2,1,0:T(8,128)} %copy-done.1, f32[]{:T(128)S(6)} %div.53, f32[]{:T(128)S(6)} %mul.354, f32[32,2,192,128]{3,2,1,0:T(8,128)} %constant_dynamic-update-slice_fusion, f32[]{:T(128)} %bitcast, ...), kind=kLoop, calls=%fused_computation.116 | loop fusion | flops 39321600 | bytes 32636940 | tf_op jit(solution)/shard_map/add | solution.py:66
  91.3 3.2 fusion.104
  94.6 1.4 copy-done.3
  95.9 1.9 collective-permute-start.4
  97.8 4.4 collective-permute-start.5
  103.6 32.0 %collective-permute-done.4 = f32[32,1,192,128]{3,2,1,0:T(8,128)} collective-permute-done((f32[32,1,192,128]{3,2,1,0:T(8,128)}, f32[32,1,192,128]{3,2,1,0:T(8,128)}, u32[]{:S(2)}, u32[]{:S(2)}) %collective-permute-start.4) | collective-permute-done | bytes 3145760 | tf_op jit(solution)/shard_map/ppermute | solution.py:19
  135.5 1.2 collective-permute-done.5
  136.7 26.0 %broadcast_divide_fusion = (f32[32,2,192,128]{3,2,1,0:T(8,128)S(1)}, f32[32,2,192,128]{3,2,1,0:T(8,128)}) fusion(f32[]{:T(128)S(6)} %mul.397, f32[32,2,192,128]{3,2,1,0:T(8,128)} %get-tuple-element.8, f32[32,2,192,128]{3,2,1,0:T(8,128)} %copy-done.3, f32[]{:T(128)} %bitcast, f32[2,192,128]{2,1,0:T(8,128)S(1)} %get-tuple-element.29, ...), kind=kLoop, calls=%fused_computation.117 | loop fusion | flops 45613056 | bytes 38928404 | tf_op jit(solution)/shard_map/div | solution.py:59
  162.7 3.8 fusion.103
  166.5 0.8 copy-done.2
  167.3 1.9 collective-permute-start.6
  169.2 4.4 collective-permute-start.7
  175.1 31.8 %collective-permute-done.6 = f32[32,1,192,128]{3,2,1,0:T(8,128)} collective-permute-done((f32[32,1,192,128]{3,2,1,0:T(8,128)}, f32[32,1,192,128]{3,2,1,0:T(8,128)}, u32[]{:S(2)}, u32[]{:S(2)}) %collective-permute-start.6) | collective-permute-done | bytes 3145760 | tf_op jit(solution)/shard_map/ppermute | solution.py:19
  207.0 1.2 collective-permute-done.7
  208.1 26.6 %multiply_add_fusion = (f32[32,2,192,128]{3,2,1,0:T(8,128)S(1)}, f32[32,2,192,128]{3,2,1,0:T(8,128)}, f32[1,32,2,192,128]{4,3,2,1,0:T(8,128)}) fusion(f32[]{:T(128)S(6)} %div.61, f32[]{:T(128)S(6)} %mul.400, f32[32,2,192,128]{3,2,1,0:T(8,128)} %get-tuple-element.6, f32[]{:T(128)S(6)} %mul.397, f32[32,2,192,128]{3,2,1,0:T(8,128)} %copy-done.2, f32[]{:T(128)} %bitcast.10, ...), kind=kLoop, calls=%fused_computation.114 | loop fusion | flops 42467328 | bytes 38928404 | tf_op jit(solution)/shard_map/add | solution.py:66
  234.7 3.8 fusion.102
  239.3 1.9 collective-permute-start.8
  241.2 4.6 collective-permute-start.9
  247.8 31.1 %collective-permute-done.8 = f32[32,1,192,128]{3,2,1,0:T(8,128)} collective-permute-done((f32[32,1,192,128]{3,2,1,0:T(8,128)}, f32[32,1,192,128]{3,2,1,0:T(8,128)}, u32[]{:S(2)}, u32[]{:S(2)}) %collective-permute-start.8) | collective-permute-done | bytes 3145760 | tf_op jit(solution)/shard_map/ppermute | solution.py:19
  278.9 1.2 collective-permute-done.9
  280.1 27.0 %fusion.47 = f32[1,32,2,192,128]{4,3,2,1,0:T(8,128)S(1)} fusion(f32[32,2,192,128]{3,2,1,0:T(8,128)} %get-tuple-element.6, f32[32,2,192,128]{3,2,1,0:T(8,128)} %get-tuple-element.4, f32[32,2,192,128]{3,2,1,0:T(8,128)} %copy-done, f32[32,1,192,128]{3,2,1,0:T(8,128)} %collective-permute-done.9, f32[32,1,192,128]{3,2,1,0:T(8,128)} %collective-permute-done.8, ...), kind=kLoop, calls=%fused_computation.65 | loop fusion | flops 48758784 | bytes 32636952 | tf_op jit(solution)/shard_map/stack | solution.py:81
  307.2 3.1 pad_maximum_fusion
  310.3 7.6 %copy.32 = f32[2,16,2,192,128]{4,2,1,0,3:T(2,128)} copy(f32[2,16,2,192,128]{4,3,2,1,0:T(8,128)S(1)} %get-tuple-element.10) | data formatting | bytes 12582912 | tf_op jit(solution)/shard_map/slice | solution.py:96
  317.9 5.3 all-to-all-start
  323.1 10.2 %copy.34 = f32[2,16,2,192,128]{4,2,1,0,3:T(2,128)} copy(f32[2,16,2,192,128]{4,3,2,1,0:T(8,128)} %get-tuple-element.9) | data formatting | bytes 12582912 | tf_op jit(solution)/shard_map/slice | solution.py:97
  333.4 51.1 %all-to-all-done = f32[2,16,2,192,128]{4,2,1,0,3:T(2,128)} async-done(((f32[2,16,2,192,128]{4,2,1,0,3:T(2,128)}), f32[2,16,2,192,128]{4,2,1,0,3:T(2,128)}, u32[]{:S(2)}, u32[]{:S(2)}) %all-to-all-start) | async-done | bytes 6291488 | tf_op jit(solution)/shard_map/all_to_all | solution.py:99
  384.5 5.2 all-to-all-start.1
  390.0 9.0 %copy.41 = f32[2,16,2,4,48,128]{5,4,2,1,3,0:T(8,128)} copy(f32[2,16,2,4,48,128]{5,2,1,0,4,3:T(2,128)} %bitcast.12) | data formatting | bytes 12582912 | tf_op jit(solution)/shard_map/all_to_all | solution.py:99
  399.0 7.5 %reshape.20 = f32[128,12288]{1,0:T(8,128)} reshape(f32[2,4,16,2,48,128]{5,4,3,2,1,0:T(8,128)} %bitcast.33) | data formatting | bytes 12582912 | tf_op jit(solution)/shard_map/reshape | solution.py:103
  406.5 25.3 %all-to-all-done.1 = f32[2,16,2,192,128]{4,2,1,0,3:T(2,128)} async-done(((f32[2,16,2,192,128]{4,2,1,0,3:T(2,128)}), f32[2,16,2,192,128]{4,2,1,0,3:T(2,128)}, u32[]{:S(2)}, u32[]{:S(2)}) %all-to-all-start.1) | async-done | bytes 6291488 | tf_op jit(solution)/shard_map/all_to_all | solution.py:100
  431.7 9.0 %copy.40 = f32[2,16,2,4,48,128]{5,4,2,1,3,0:T(8,128)} copy(f32[2,16,2,4,48,128]{5,2,1,0,4,3:T(2,128)} %bitcast.15) | data formatting | bytes 12582912 | tf_op jit(solution)/shard_map/all_to_all | solution.py:100
  440.8 7.4 %reshape.21 = f32[128,12288]{1,0:T(8,128)} reshape(f32[2,4,16,2,48,128]{5,4,3,2,1,0:T(8,128)} %bitcast.35) | data formatting | bytes 12582912 | tf_op jit(solution)/shard_map/reshape | solution.py:104
  448.2 8.8 %fusion.109 = f32[128,128]{1,0:T(8,128)} fusion(f32[128,12288]{1,0:T(8,128)} %reshape.20, f32[128,12288]{1,0:T(8,128)} %reshape.21), kind=kOutput, calls=%fused_computation.151 | convolution fusion | flops 2415919104 | bytes 12648448 | tf_op jit(solution)/shard_map/dot_general | solution.py:105
  457.1 111.1 %all-gather.3.cloned.1.call-done = f32[16384,128]{1,0:T(8,128)} async-done(((f32[128,128]{1,0:T(8,128)}), f32[16384,128]{1,0:T(8,128)}) %all-gather.3.cloned.1.call-update) | async-done | bytes 8388624 | tf_op jit(solution)/shard_map/all_gather | solution.py:114
  568.1 3.8 reduce_sum.9
  (23 shorter events, 4.1 us)
Async XLA Ops:
  7.2 8.6 %copy-start.5 = (f32[16,2,192,128]{3,2,1,0:T(8,128)S(1)}, f32[16,2,192,128]{3,2,1,0:T(8,128)}, u32[]{:S(2)}) copy-start(f32[16,2,192,128]{3,2,1,0:T(8,128)} %param.6) | copy-start | bytes 9437188
  20.9 4.6 copy-start.1
  20.9 11.4 %copy-start.7 = (f32[8]{0:T(128)S(1)}, f32[8]{0:T(128)}, u32[]{:S(2)}) copy-start(f32[8]{0:T(128)} %param.8) | copy-start | bytes 100
  20.9 12.1 %copy-start.6 = (s32[2,192,128]{2,1,0:T(8,128)S(1)}, s32[2,192,128]{2,1,0:T(8,128)}, u32[]{:S(2)}) copy-start(s32[2,192,128]{2,1,0:T(8,128)} %param.7) | copy-start | bytes 589828
  25.4 42.5 %collective-permute-start.1 = (f32[32,1,192,128]{3,2,1,0:T(8,128)}, f32[32,1,192,128]{3,2,1,0:T(8,128)}, u32[]{:S(2)}, u32[]{:S(2)}) collective-permute-start(f32[32,1,192,128]{3,2,1,0:T(8,128)} %get-tuple-element.22), channel_id=1, source_target_pairs={{4,0},{8,4},{12,8},{16,12},{20,16},{24,20},{28,24},{32,28},{36,32}... | collective-permute-start | bytes 9437192 | tf_op jit(solution)/shard_map/ppermute | solution.py:19
  28.8 39.2 %collective-permute-start.3 = (f32[32,1,192,128]{3,2,1,0:T(8,128)}, f32[32,1,192,128]{3,2,1,0:T(8,128)}, u32[]{:S(2)}, u32[]{:S(2)}) collective-permute-start(f32[32,1,192,128]{3,2,1,0:T(8,128)} %get-tuple-element.23), channel_id=1, source_target_pairs={{0,4},{4,8},{8,12},{12,16},{16,20},{20,24},{24,28},{28,32},{32,36}... | collective-permute-start | bytes 9437192 | tf_op jit(solution)/shard_map/ppermute | solution.py:16
  38.2 28.4 %collective-permute-start = (f32[1,192,128]{2,1,0:T(8,128)S(1)}, f32[1,192,128]{2,1,0:T(8,128)S(1)}, u32[]{:S(2)}, u32[]{:S(2)}) collective-permute-start(f32[1,192,128]{2,1,0:T(8,128)S(1)} %get-tuple-element.30), channel_id=1, source_target_pairs={{4,0},{8,4},{12,8},{16,12},{20,16},{24,20},{28,24},{32,28},{36,32}... | collective-permute-start | bytes 294920 | tf_op jit(solution)/shard_map/ppermute | solution.py:19
  40.7 27.1 %collective-permute-start.2 = (f32[1,192,128]{2,1,0:T(8,128)S(1)}, f32[1,192,128]{2,1,0:T(8,128)S(1)}, u32[]{:S(2)}, u32[]{:S(2)}) collective-permute-start(f32[1,192,128]{2,1,0:T(8,128)S(1)} %get-tuple-element.31), channel_id=1, source_target_pairs={{0,4},{4,8},{8,12},{12,16},{16,20},{20,24},{24,28},{28,32},{32,36}... | collective-permute-start | bytes 294920 | tf_op jit(solution)/shard_map/ppermute | solution.py:16
  91.3 4.6 copy-start.3
  95.9 39.6 %collective-permute-start.4 = (f32[32,1,192,128]{3,2,1,0:T(8,128)}, f32[32,1,192,128]{3,2,1,0:T(8,128)}, u32[]{:S(2)}, u32[]{:S(2)}) collective-permute-start(f32[32,1,192,128]{3,2,1,0:T(8,128)} %get-tuple-element.20), channel_id=1, source_target_pairs={{4,0},{8,4},{12,8},{16,12},{20,16},{24,20},{28,24},{32,28},{36,32}... | collective-permute-start | bytes 9437192 | tf_op jit(solution)/shard_map/ppermute | solution.py:19
  97.8 38.9 %collective-permute-start.5 = (f32[32,1,192,128]{3,2,1,0:T(8,128)}, f32[32,1,192,128]{3,2,1,0:T(8,128)}, u32[]{:S(2)}, u32[]{:S(2)}) collective-permute-start(f32[32,1,192,128]{3,2,1,0:T(8,128)} %get-tuple-element.21), channel_id=1, source_target_pairs={{0,4},{4,8},{8,12},{12,16},{16,20},{20,24},{24,28},{28,32},{32,36}... | collective-permute-start | bytes 9437192 | tf_op jit(solution)/shard_map/ppermute | solution.py:16
  162.7 4.6 copy-start.2
  167.3 39.6 %collective-permute-start.6 = (f32[32,1,192,128]{3,2,1,0:T(8,128)}, f32[32,1,192,128]{3,2,1,0:T(8,128)}, u32[]{:S(2)}, u32[]{:S(2)}) collective-permute-start(f32[32,1,192,128]{3,2,1,0:T(8,128)} %get-tuple-element.18), channel_id=1, source_target_pairs={{4,0},{8,4},{12,8},{16,12},{20,16},{24,20},{28,24},{32,28},{36,32}... | collective-permute-start | bytes 9437192 | tf_op jit(solution)/shard_map/ppermute | solution.py:19
  169.2 38.9 %collective-permute-start.7 = (f32[32,1,192,128]{3,2,1,0:T(8,128)}, f32[32,1,192,128]{3,2,1,0:T(8,128)}, u32[]{:S(2)}, u32[]{:S(2)}) collective-permute-start(f32[32,1,192,128]{3,2,1,0:T(8,128)} %get-tuple-element.19), channel_id=1, source_target_pairs={{0,4},{4,8},{8,12},{12,16},{16,20},{20,24},{24,28},{28,32},{32,36}... | collective-permute-start | bytes 9437192 | tf_op jit(solution)/shard_map/ppermute | solution.py:16
  234.7 4.6 copy-start
  239.3 39.6 %collective-permute-start.8 = (f32[32,1,192,128]{3,2,1,0:T(8,128)}, f32[32,1,192,128]{3,2,1,0:T(8,128)}, u32[]{:S(2)}, u32[]{:S(2)}) collective-permute-start(f32[32,1,192,128]{3,2,1,0:T(8,128)} %get-tuple-element.15), channel_id=1, source_target_pairs={{4,0},{8,4},{12,8},{16,12},{20,16},{24,20},{28,24},{32,28},{36,32}... | collective-permute-start | bytes 9437192 | tf_op jit(solution)/shard_map/ppermute | solution.py:19
  241.2 38.9 %collective-permute-start.9 = (f32[32,1,192,128]{3,2,1,0:T(8,128)}, f32[32,1,192,128]{3,2,1,0:T(8,128)}, u32[]{:S(2)}, u32[]{:S(2)}) collective-permute-start(f32[32,1,192,128]{3,2,1,0:T(8,128)} %get-tuple-element.16), channel_id=1, source_target_pairs={{0,4},{4,8},{8,12},{12,16},{16,20},{20,24},{24,28},{28,32},{32,36}... | collective-permute-start | bytes 9437192 | tf_op jit(solution)/shard_map/ppermute | solution.py:16
  280.1 27.0 %copy-start.4 = (f32[1,32,2,192,128]{4,3,2,1,0:T(8,128)S(1)}, f32[1,32,2,192,128]{4,3,2,1,0:T(8,128)}, u32[]{:S(2)}) copy-start(f32[1,32,2,192,128]{4,3,2,1,0:T(8,128)} %get-tuple-element.17) | copy-start | bytes 18874372
  317.9 66.6 %all-to-all-start = ((f32[2,16,2,192,128]{4,2,1,0,3:T(2,128)}), f32[2,16,2,192,128]{4,2,1,0,3:T(2,128)}, u32[]{:S(2)}, u32[]{:S(2)}) async-start(f32[2,16,2,192,128]{4,2,1,0,3:T(2,128)} %copy.32), calls=%async_computation | async-start | bytes 12582912 | tf_op jit(solution)/shard_map/all_to_all | solution.py:99
  384.5 47.3 %all-to-all-start.1 = ((f32[2,16,2,192,128]{4,2,1,0,3:T(2,128)}), f32[2,16,2,192,128]{4,2,1,0,3:T(2,128)}, u32[]{:S(2)}, u32[]{:S(2)}) async-start(f32[2,16,2,192,128]{4,2,1,0,3:T(2,128)} %copy.34), calls=%async_computation.1 | async-start | bytes 12582912 | tf_op jit(solution)/shard_map/all_to_all | solution.py:100
  389.7 178.4 %all-gather.3.cloned.1.call-start = ((), (), s32[]{:S(2)}) async-start(), calls=%async_computation.2 | async-start | bytes 8454144 | tf_op jit(solution)/shard_map/all_gather | solution.py:114
Sparse Core Ops, SparseCore 0:
  457.2 110.8 all-gather.2
